TPU v7x, 512 devices: a whole 4x4x16 slice. The times are simulated.
512 devices in a mesh: rep: 8 (over z_lo), blk: 64 (over y, z_hi, x, core).
Axes of the slice: x: 4, y: 4, z: 16 (z_hi: 2, z_lo: 8; z = z_hi * 8 + z_lo), core: 2. Of those that a mesh axis runs over, the one named last changes fastest.
Arguments:
- features: bfloat16 [65536, 256], P(('rep', 'blk')), may hold values from -6 to 6
- weight: bfloat16 [256, 256], replicated, may hold values from -0.375 to 0.375
- cotangent: bfloat16 [65536, 256], P(('rep', 'blk')), may hold values from -6 to 6
- tile_row: int32 [8, 64, 8, 4], P('rep', 'blk'), may hold values from 0 to 511, as said below
- tile_col: int32 [8, 64, 8, 4], P('rep', 'blk'), may hold values from 0 to 511, as said below
- tile_count: int32 [8, 64, 8], P('rep', 'blk'), may hold values from 1 to 4, as said below
- tile_vals: bfloat16 [8, 64, 8, 4, 128, 128], P('rep', 'blk'), may hold values from 0 to 0.015625
Outputs:
- activations: bfloat16 [65536, 256], P(('rep', 'blk'))
- weight_grad: float32 [256, 256], replicated
- feature_grad: bfloat16 [65536, 256], P(('rep', 'blk'))
Inputs may be any that keep to these rules, and one draw needn't show every extreme that they name: In slot (r, p, t, k) the row block lies in row panel p: p * 8 <= tile_row < (p + 1) * 8. The live slots of one (r, p, t) hold distinct (tile_row, tile_col) pairs. In slot (r, p, t, k) the column block lies in column panel q = (p - 8 * r - t) mod 64: q * 8 <= tile_col < (q + 1) * 8. Slots with k >= tile_count[r, p, t] are unused. `tile_count`: the value 4 occurs in every draw.
All inputs are finite; a program needn't handle non-finite values.
Results may differ from a plain program's by a relative error of at most 0.018.
Values may be sent and summed in bfloat16 or wider, within the bound.
A program may use at most 64 MiB of HBM per device.

v0:
```python
import math
import jax
import jax.numpy as jnp
from jax import lax
from jax.sharding import PartitionSpec as P


def passed_along(array, axis, by):
    peers = lax.axis_size(axis)
    return lax.ppermute(array, axis, [(i, (i + by) % peers) for i in range(peers)])


def silu_slope(values):
    sigmoid_part = jax.nn.sigmoid(values)
    return sigmoid_part * (1.0 + values * (1.0 - sigmoid_part))


def block_select(block_ids, live_slots, blocks):
    levels = lax.broadcasted_iota(jnp.int32, (block_ids.shape[0], blocks), 1)
    return ((block_ids[:, None] == levels) & live_slots[:, None]).astype(jnp.float32)


def forward_terms(panel, tiles, rows_local, cols_local, live_slots):
    picked = jnp.take(panel, cols_local, axis=0)
    product = jnp.einsum("kij,kjf->kif", tiles, picked, preferred_element_type=jnp.float32)
    select_rows = block_select(rows_local, live_slots, panel.shape[0])
    return jnp.einsum("kc,kif->cif", select_rows, product, precision=lax.Precision.HIGHEST)


def backward_terms(panel, tiles, rows_local, cols_local, live_slots):
    picked = jnp.take(panel, rows_local, axis=0)
    product = jnp.einsum("kji,kjf->kif", tiles, picked, preferred_element_type=jnp.float32)
    select_cols = block_select(cols_local, live_slots, panel.shape[0])
    return jnp.einsum("kc,kif->cif", select_cols, product, precision=lax.Precision.HIGHEST)


def on_device(features, weight, cotangent, tile_row, tile_col, tile_count, tile_vals):
    slab_rows, width = features.shape
    groups = lax.axis_size("rep")
    panels = lax.axis_size("blk")
    steps = panels // groups
    tile_size = tile_vals.shape[-1]
    blocks = groups * slab_rows // tile_size
    slots = tile_vals.shape[3]
    member = lax.axis_index("rep")
    rows_local = tile_row[0, 0] % blocks
    cols_local = tile_col[0, 0] % blocks
    live_slots = lax.broadcasted_iota(jnp.int32, (steps, slots), 1) < tile_count[0, 0][:, None]
    tiles = tile_vals[0, 0]
    total_nodes = slab_rows * groups * panels

    def forward_at(panel, index):
        return forward_terms(
            panel, tiles[index], rows_local[index], cols_local[index], live_slots[index]
        )

    def backward_at(panel, index):
        return backward_terms(
            panel, tiles[index], rows_local[index], cols_local[index], live_slots[index]
        )

    panel = lax.all_gather(features, "rep", axis=0, tiled=True)
    for level in range(groups.bit_length() - 1):
        moved = passed_along(panel, "blk", steps << level)
        panel = jnp.where(member >> level & 1 == 1, moved, panel)
    panel = panel.reshape(blocks, tile_size, width)
    partial_value = forward_at(panel, 0)
    for index in range(1, steps):
        panel = passed_along(panel, "blk", 1)
        partial_value = partial_value + forward_at(panel, index)
    row_part = lax.psum_scatter(
        partial_value.reshape(-1, width), "rep", scatter_dimension=0, tiled=True
    )
    aggregated = row_part.astype(jnp.bfloat16)
    preact = jnp.dot(aggregated, weight, preferred_element_type=jnp.float32)
    activations = jax.nn.silu(preact).astype(jnp.bfloat16)
    slope_grad = (cotangent.astype(jnp.float32) * silu_slope(preact)).astype(jnp.bfloat16)
    local_grad = jnp.dot(aggregated.T, slope_grad, preferred_element_type=jnp.float32)
    weight_grad = lax.psum(local_grad, ("rep", "blk")) * (1.0 / math.sqrt(total_nodes))
    back_rows = jnp.dot(slope_grad, weight.T, preferred_element_type=jnp.float32).astype(
        jnp.bfloat16
    )
    grad_panel = lax.all_gather(back_rows, "rep", axis=0, tiled=True).reshape(
        blocks, tile_size, width
    )
    carried = backward_at(grad_panel, steps - 1)
    for index in range(steps - 2, -1, -1):
        carried = passed_along(carried, "blk", -1) + backward_at(grad_panel, index)
    for level in range(groups.bit_length() - 1):
        moved = passed_along(carried.astype(jnp.bfloat16), "blk", -(steps << level)).astype(
            carried.dtype
        )
        carried = jnp.where(member >> level & 1 == 1, moved, carried)
    column_part = lax.psum_scatter(
        carried.reshape(-1, width).astype(jnp.bfloat16), "rep", scatter_dimension=0, tiled=True
    )
    return (activations, weight_grad, column_part)


def solution(mesh):
    return jax.shard_map(
        on_device,
        mesh=mesh,
        in_specs=(
            P(("rep", "blk"), None),
            P(),
            P(("rep", "blk"), None),
            P("rep", "blk", None, None),
            P("rep", "blk", None, None),
            P("rep", "blk", None),
            P("rep", "blk", None, None, None, None),
        ),
        out_specs=(P(("rep", "blk"), None), P(), P(("rep", "blk"), None)),
        check_vma=False,
    )
```

profile of v0, /device:TPU:4, one launch (start us, length us, event | category | flops | bytes accessed | tf_op | source)
XLA Modules:
  0.0 1385.4 jit_solution(2886629018027375451)
XLA Ops:
  7.2 50.9 %all_gather.6 = bf16[1024,256]{1,0:T(8,128)(2,1)S(1)} all-gather(bf16[128,256]{1,0:T(8,128)(2,1)} %param.9), channel_id=1, replica_groups=mesh['rep'=8,'blk'=64] {'rep'}, dimensions={0}, use_global_device_ids=true | all-gather | bytes 589824 | tf_op jit(solution)/shard_map/all_gather | solution.py:62
  58.1 32.2 %collective-permute-start = (bf16[1024,256]{1,0:T(8,128)(2,1)S(1)}, bf16[1024,256]{1,0:T(8,128)(2,1)S(1)}, u32[]{:S(2)}, u32[]{:S(2)}) collective-permute-start(bf16[1024,256]{1,0:T(8,128)(2,1)S(1)} %all_gather.6), channel_id=1, source_target_pairs={{0,8},{1,9},{2,10},{3,11},{4,12},{5,13},{6,14},{7,15},{8,16},{9,17... | collective-permute-start | bytes 1572872 | tf_op jit(solution)/shard_map/ppermute | solution.py:10
  91.9 19.1 %collective-permute-done = bf16[1024,256]{1,0:T(8,128)(2,1)S(1)} collective-permute-done((bf16[1024,256]{1,0:T(8,128)(2,1)S(1)}, bf16[1024,256]{1,0:T(8,128)(2,1)S(1)}, u32[]{:S(2)}, u32[]{:S(2)}) %collective-permute-start) | collective-permute-done | bytes 524320 | tf_op jit(solution)/shard_map/ppermute | solution.py:10
  113.0 13.2 collective-permute-done.1
  129.5 11.4 collective-permute-done.2
  185.0 19.4 %collective-permute-start.7 = (bf16[8,128,256]{2,1,0:T(8,128)(2,1)}, bf16[8,128,256]{2,1,0:T(8,128)(2,1)}, u32[]{:S(2)}, u32[]{:S(2)}) collective-permute-start(bf16[8,128,256]{2,1,0:T(8,128)(2,1)} %collective-permute-done.6), channel_id=1, source_target_pairs={{0,1},{1,2},{2,3},{3,4},{4,5},{5,6},{6,7},{7,8},{8,9},{9,10},{10,1... | collective-permute-start | bytes 1572872 | tf_op jit(solution)/shard_map/ppermute | solution.py:10
  209.0 20.9 %collective-permute-start.8 = (bf16[8,128,256]{2,1,0:T(8,128)(2,1)}, bf16[8,128,256]{2,1,0:T(8,128)(2,1)}, u32[]{:S(2)}, u32[]{:S(2)}) collective-permute-start(bf16[8,128,256]{2,1,0:T(8,128)(2,1)} %collective-permute-done.7), channel_id=1, source_target_pairs={{0,1},{1,2},{2,3},{3,4},{4,5},{5,6},{6,7},{7,8},{8,9},{9,10},{10,1... | collective-permute-start | bytes 1572872 | tf_op jit(solution)/shard_map/ppermute | solution.py:10
  234.6 24.9 %collective-permute-start.9 = (bf16[8,128,256]{2,1,0:T(8,128)(2,1)}, bf16[8,128,256]{2,1,0:T(8,128)(2,1)}, u32[]{:S(2)}, u32[]{:S(2)}) collective-permute-start(bf16[8,128,256]{2,1,0:T(8,128)(2,1)} %collective-permute-done.8), channel_id=1, source_target_pairs={{0,1},{1,2},{2,3},{3,4},{4,5},{5,6},{6,7},{7,8},{8,9},{9,10},{10,1... | collective-permute-start | bytes 1572872 | tf_op jit(solution)/shard_map/ppermute | solution.py:10
  269.5 126.2 %reduce-scatter.3.cloned.1.call-done = f32[128,256]{1,0:T(8,128)} async-done(((f32[1024,256]{1,0:T(8,128)}), f32[128,256]{1,0:T(8,128)}) %reduce-scatter.3.cloned.1.call-update) | async-done | bytes 131088 | tf_op jit(solution)/shard_map/reduce_scatter | solution.py:71
  397.6 47.7 %all_gather.7 = bf16[1024,256]{1,0:T(8,128)(2,1)S(1)} all-gather(bf16[128,256]{1,0:T(8,128)(2,1)S(1)} %convolution_convert_fusion), channel_id=1, replica_groups=mesh['rep'=8,'blk'=64] {'rep'}, dimensions={0}, use_global_device_ids=true | all-gather | bytes 589824 | tf_op jit(solution)/shard_map/all_gather | solution.py:83
  451.5 11.4 collective-permute-done.10
  471.7 10.6 collective-permute-done.11
  490.6 10.6 collective-permute-done.12
  509.5 20.5 %collective-permute-done.13 = f32[8,128,256]{2,0,1:T(8,128)} collective-permute-done((f32[8,128,256]{2,0,1:T(8,128)}, f32[8,128,256]{2,0,1:T(8,128)}, u32[]{:S(2)}, u32[]{:S(2)}) %collective-permute-start.13) | collective-permute-done | bytes 1048608 | tf_op jit(solution)/shard_map/ppermute | solution.py:10
  536.3 32.1 %collective-permute-done.14 = f32[8,128,256]{2,0,1:T(8,128)} collective-permute-done((f32[8,128,256]{2,0,1:T(8,128)}, f32[8,128,256]{2,0,1:T(8,128)}, u32[]{:S(2)}, u32[]{:S(2)}) %collective-permute-start.14) | collective-permute-done | bytes 1048608 | tf_op jit(solution)/shard_map/ppermute | solution.py:10
  574.8 38.3 %collective-permute-done.15 = f32[8,128,256]{2,0,1:T(8,128)} collective-permute-done((f32[8,128,256]{2,0,1:T(8,128)}, f32[8,128,256]{2,0,1:T(8,128)}, u32[]{:S(2)}, u32[]{:S(2)}) %collective-permute-start.15) | collective-permute-done | bytes 1048608 | tf_op jit(solution)/shard_map/ppermute | solution.py:10
  618.4 41.4 %collective-permute-done.16 = f32[8,128,256]{2,0,1:T(8,128)} collective-permute-done((f32[8,128,256]{2,0,1:T(8,128)S(1)}, f32[8,128,256]{2,0,1:T(8,128)}, u32[]{:S(2)}, u32[]{:S(2)}) %collective-permute-start.16) | collective-permute-done | bytes 1048608 | tf_op jit(solution)/shard_map/ppermute | solution.py:10
  661.2 11.2 collective-permute-start.17
  672.5 8.5 collective-permute-done.17
  681.1 6.7 collective-permute-start.18
  687.8 6.7 collective-permute-done.18
  699.6 7.7 collective-permute-done.19
  708.5 606.6 %all-reduce.2.cloned.1.call-done = f32[256,256]{1,0:T(8,128)} async-done(((f32[256,256]{1,0:T(8,128)}), f32[256,256]{1,0:T(8,128)}) %all-reduce.2.cloned.1.call-update) | async-done | bytes 262160 | tf_op jit(solution)/shard_map/psum | solution.py:79
  1316.8 62.1 %reduce-scatter.5.cloned.1.call-done = bf16[128,256]{1,0:T(8,128)(2,1)} async-done(((bf16[1024,256]{1,0:T(8,128)(2,1)}), bf16[128,256]{1,0:T(8,128)(2,1)}) %reduce-scatter.5.cloned.1.call-update) | async-done | bytes 65552 | tf_op jit(solution)/shard_map/reduce_scatter | solution.py:94
  (179 shorter events, 129.9 us)
Async XLA Ops:
  7.2 388.5 %copy-start = (bf16[256,256]{1,0:T(8,128)(2,1)S(1)}, bf16[256,256]{1,0:T(8,128)(2,1)}, u32[]{:S(2)}) copy-start(bf16[256,256]{1,0:T(8,128)(2,1)} %param.10) | copy-start | bytes 393220
  7.2 388.5 %reduce-scatter.3.cloned.1.call-start = ((), (), s32[]{:S(2)}) async-start(), calls=%async_computation.2 | async-start | bytes 1179648 | tf_op jit(solution)/shard_map/reduce_scatter | solution.py:71
  58.1 52.8 %collective-permute-start = (bf16[1024,256]{1,0:T(8,128)(2,1)S(1)}, bf16[1024,256]{1,0:T(8,128)(2,1)S(1)}, u32[]{:S(2)}, u32[]{:S(2)}) collective-permute-start(bf16[1024,256]{1,0:T(8,128)(2,1)S(1)} %all_gather.6), channel_id=1, source_target_pairs={{0,8},{1,9},{2,10},{3,11},{4,12},{5,13},{6,14},{7,15},{8,16},{9,17... | collective-permute-start | bytes 1572872 | tf_op jit(solution)/shard_map/ppermute | solution.py:10
  111.0 15.2 %collective-permute-start.1 = (bf16[1024,256]{1,0:T(8,128)(2,1)S(1)}, bf16[1024,256]{1,0:T(8,128)(2,1)S(1)}, u32[]{:S(2)}, u32[]{:S(2)}) collective-permute-start(bf16[1024,256]{1,0:T(8,128)(2,1)S(1)} %broadcast_select_fusion), channel_id=1, source_target_pairs={{0,16},{1,17},{2,18},{3,19},{4,20},{5,21},{6,22},{7,23},{8,24},{9,... | collective-permute-start | bytes 1572872 | tf_op jit(solution)/shard_map/ppermute | solution.py:10
  126.3 14.6 %collective-permute-start.2 = (bf16[1024,256]{1,0:T(8,128)(2,1)S(1)}, bf16[1024,256]{1,0:T(8,128)(2,1)S(1)}, u32[]{:S(2)}, u32[]{:S(2)}) collective-permute-start(bf16[1024,256]{1,0:T(8,128)(2,1)S(1)} %broadcast_select_fusion.1), channel_id=1, source_target_pairs={{0,32},{1,33},{2,34},{3,35},{4,36},{5,37},{6,38},{7,39},{8,40},{9,... | collective-permute-start | bytes 1572872 | tf_op jit(solution)/shard_map/ppermute | solution.py:10
  141.7 10.8 collective-permute-start.3
  152.5 10.8 collective-permute-start.4
  163.3 10.8 collective-permute-start.5
  174.2 10.8 collective-permute-start.6
  185.0 24.1 %collective-permute-start.7 = (bf16[8,128,256]{2,1,0:T(8,128)(2,1)}, bf16[8,128,256]{2,1,0:T(8,128)(2,1)}, u32[]{:S(2)}, u32[]{:S(2)}) collective-permute-start(bf16[8,128,256]{2,1,0:T(8,128)(2,1)} %collective-permute-done.6), channel_id=1, source_target_pairs={{0,1},{1,2},{2,3},{3,4},{4,5},{5,6},{6,7},{7,8},{8,9},{9,10},{10,1... | collective-permute-start | bytes 1572872 | tf_op jit(solution)/shard_map/ppermute | solution.py:10
  209.0 25.6 %collective-permute-start.8 = (bf16[8,128,256]{2,1,0:T(8,128)(2,1)}, bf16[8,128,256]{2,1,0:T(8,128)(2,1)}, u32[]{:S(2)}, u32[]{:S(2)}) collective-permute-start(bf16[8,128,256]{2,1,0:T(8,128)(2,1)} %collective-permute-done.7), channel_id=1, source_target_pairs={{0,1},{1,2},{2,3},{3,4},{4,5},{5,6},{6,7},{7,8},{8,9},{9,10},{10,1... | collective-permute-start | bytes 1572872 | tf_op jit(solution)/shard_map/ppermute | solution.py:10
  234.6 29.6 %collective-permute-start.9 = (bf16[8,128,256]{2,1,0:T(8,128)(2,1)}, bf16[8,128,256]{2,1,0:T(8,128)(2,1)}, u32[]{:S(2)}, u32[]{:S(2)}) collective-permute-start(bf16[8,128,256]{2,1,0:T(8,128)(2,1)} %collective-permute-done.8), channel_id=1, source_target_pairs={{0,1},{1,2},{2,3},{3,4},{4,5},{5,6},{6,7},{7,8},{8,9},{9,10},{10,1... | collective-permute-start | bytes 1572872 | tf_op jit(solution)/shard_map/ppermute | solution.py:10
  269.2 1045.9 %all-reduce.2.cloned.1.call-start = ((), (), s32[]{:S(2)}) async-start(), calls=%async_computation.3 | async-start | bytes 524288 | tf_op jit(solution)/shard_map/psum | solution.py:79
  448.4 14.5 %collective-permute-start.10 = (f32[8,128,256]{2,0,1:T(8,128)}, f32[8,128,256]{2,0,1:T(8,128)}, u32[]{:S(2)}, u32[]{:S(2)}) collective-permute-start(f32[8,128,256]{2,0,1:T(8,128)} %fusion.14), channel_id=1, source_target_pairs={{0,63},{1,0},{2,1},{3,2},{4,3},{5,4},{6,5},{7,6},{8,7},{9,8},{10,9... | collective-permute-start | bytes 3145736 | tf_op jit(solution)/shard_map/ppermute | solution.py:10
  465.9 16.4 %collective-permute-start.11 = (f32[8,128,256]{2,0,1:T(8,128)}, f32[8,128,256]{2,0,1:T(8,128)}, u32[]{:S(2)}, u32[]{:S(2)}) collective-permute-start(f32[8,128,256]{2,0,1:T(8,128)} %convolution_add_fusion), channel_id=1, source_target_pairs={{0,63},{1,0},{2,1},{3,2},{4,3},{5,4},{6,5},{7,6},{8,7},{9,8},{10,9... | collective-permute-start | bytes 3145736 | tf_op jit(solution)/shard_map/ppermute | solution.py:10
  484.8 16.4 %collective-permute-start.12 = (f32[8,128,256]{2,0,1:T(8,128)}, f32[8,128,256]{2,0,1:T(8,128)}, u32[]{:S(2)}, u32[]{:S(2)}) collective-permute-start(f32[8,128,256]{2,0,1:T(8,128)} %add.81), channel_id=1, source_target_pairs={{0,63},{1,0},{2,1},{3,2},{4,3},{5,4},{6,5},{7,6},{8,7},{9,8},{10,9... | collective-permute-start | bytes 3145736 | tf_op jit(solution)/shard_map/ppermute | solution.py:10
  503.7 26.3 %collective-permute-start.13 = (f32[8,128,256]{2,0,1:T(8,128)}, f32[8,128,256]{2,0,1:T(8,128)}, u32[]{:S(2)}, u32[]{:S(2)}) collective-permute-start(f32[8,128,256]{2,0,1:T(8,128)} %add.82), channel_id=1, source_target_pairs={{0,63},{1,0},{2,1},{3,2},{4,3},{5,4},{6,5},{7,6},{8,7},{9,8},{10,9... | collective-permute-start | bytes 3145736 | tf_op jit(solution)/shard_map/ppermute | solution.py:10
  532.4 36.0 %collective-permute-start.14 = (f32[8,128,256]{2,0,1:T(8,128)}, f32[8,128,256]{2,0,1:T(8,128)}, u32[]{:S(2)}, u32[]{:S(2)}) collective-permute-start(f32[8,128,256]{2,0,1:T(8,128)} %add.83), channel_id=1, source_target_pairs={{0,63},{1,0},{2,1},{3,2},{4,3},{5,4},{6,5},{7,6},{8,7},{9,8},{10,9... | collective-permute-start | bytes 3145736 | tf_op jit(solution)/shard_map/ppermute | solution.py:10
  570.8 42.3 %collective-permute-start.15 = (f32[8,128,256]{2,0,1:T(8,128)}, f32[8,128,256]{2,0,1:T(8,128)}, u32[]{:S(2)}, u32[]{:S(2)}) collective-permute-start(f32[8,128,256]{2,0,1:T(8,128)} %add.84), channel_id=1, source_target_pairs={{0,63},{1,0},{2,1},{3,2},{4,3},{5,4},{6,5},{7,6},{8,7},{9,8},{10,9... | collective-permute-start | bytes 3145736 | tf_op jit(solution)/shard_map/ppermute | solution.py:10
  614.5 45.3 %collective-permute-start.16 = (f32[8,128,256]{2,0,1:T(8,128)S(1)}, f32[8,128,256]{2,0,1:T(8,128)}, u32[]{:S(2)}, u32[]{:S(2)}) collective-permute-start(f32[8,128,256]{2,0,1:T(8,128)S(1)} %add.85), channel_id=1, source_target_pairs={{0,63},{1,0},{2,1},{3,2},{4,3},{5,4},{6,5},{7,6},{8,7},{9,8},{10,9... | collective-permute-start | bytes 3145736 | tf_op jit(solution)/shard_map/ppermute | solution.py:10
  661.2 19.8 %collective-permute-start.17 = (bf16[8,128,256]{2,0,1:T(8,128)(2,1)S(1)}, bf16[8,128,256]{2,0,1:T(8,128)(2,1)S(1)}, u32[]{:S(2)}, u32[]{:S(2)}) collective-permute-start(bf16[8,128,256]{2,0,1:T(8,128)(2,1)S(1)} %add.86), channel_id=1, source_target_pairs={{0,56},{1,57},{2,58},{3,59},{4,60},{5,61},{6,62},{7,63},{8,0},{9,1... | collective-permute-start | bytes 1572872 | tf_op jit(solution)/shard_map/ppermute | solution.py:10
  681.1 13.3 collective-permute-start.18
  694.7 12.6 collective-permute-start.19
  699.5 679.4 %reduce-scatter.5.cloned.1.call-start = ((), (), s32[]{:S(2)}) async-start(), calls=%async_computation.4 | async-start | bytes 589824 | tf_op jit(solution)/shard_map/reduce_scatter | solution.py:94
  (11 other events, 251.8 us)
Sparse Core Ops, SparseCore 0:
  269.3 126.3 reduce-scatter.2
  699.6 615.4 all-reduce.1
  1318.7 60.1 reduce-scatter.4
where the time goes:
time: 1390 us
  waiting for transfers between devices  1050 us (76%)
  starting transfers between devices  151 us (11%)
  blocking collectives  98.6 us (7%)
  matrix products  30.3 us (2%)
  local copies, waits for them, and re-layouts  29.1 us (2%)
  other arithmetic  16.2 us (1%)
  between operations  14.8 us (1%)
    psum x1, waiting for transfers between devices, on_device(): lax.psum(local_grad, ('rep', 'blk')) * (1.0 / math.sqrt(total_nodes))  607 us
    ppermute x20, waiting for transfers between devices, passed_along(): lax.ppermute(array, axis, [(i, (i + by) % peers) for i in range(peers)])  251 us
    ppermute x20, starting transfers between devices, passed_along(): lax.ppermute(array, axis, [(i, (i + by) % peers) for i in range(peers)])  150 us
    reduce_scatter x1, waiting for transfers between devices, on_device(): lax.psum_scatter(partial_value.reshape(-1, width), 'rep', scatter_dimensi...  126 us
    reduce_scatter x1, waiting for transfers between devices, on_device(): lax.psum_scatter(carried.reshape(-1, width).astype(jnp.bfloat16), 'rep',...  62.1 us
    all_gather x1, blocking collectives, on_device(): panel = lax.all_gather(features, 'rep', axis=0, tiled=True)  50.9 us
    all_gather x1, blocking collectives, on_device(): lax.all_gather(back_rows, 'rep', axis=0, tiled=True)  47.7 us
  transfers between devices with their start and end apart: 23, of which 20 were waited for; matrix products, arithmetic and copies ran while one was open for 3% of the time, Pallas kernels for 0%

commit v1 on v0

--- a/solution.py
+++ b/solution.py
@@ -76,7 +76,7 @@
     activations = jax.nn.silu(preact).astype(jnp.bfloat16)
     slope_grad = (cotangent.astype(jnp.float32) * silu_slope(preact)).astype(jnp.bfloat16)
     local_grad = jnp.dot(aggregated.T, slope_grad, preferred_element_type=jnp.float32)
-    weight_grad = lax.psum(local_grad, ("rep", "blk")) * (1.0 / math.sqrt(total_nodes))
+    weight_grad = lax.psum(lax.psum(local_grad, "rep"), "blk") * (1.0 / math.sqrt(total_nodes))
     back_rows = jnp.dot(slope_grad, weight.T, preferred_element_type=jnp.float32).astype(
         jnp.bfloat16
     )

time: 1390 us -> 2080 us (1.50)
  the two profiles are of different devices: /device:TPU:4 before, /device:TPU:6 now
where the time goes in v1:
time: 2080 us
  waiting for transfers between devices  1690 us (81%)
  starting transfers between devices  198 us (10%)
  blocking collectives  98.6 us (5%)
  matrix products  30.3 us (1%)
  local copies, waits for them, and re-layouts  29.1 us (1%)
    psum x1, waiting for transfers between devices, on_device(): lax.psum(lax.psum(local_grad, 'rep'), 'blk')  1000 us
    ppermute x20, waiting for transfers between devices, passed_along(): lax.ppermute(array, axis, [(i, (i + by) % peers) for i in range(peers)])  308 us
    psum x1, waiting for transfers between devices, on_device(): lax.psum(local_grad, 'rep')  205 us
    ppermute x20, starting transfers between devices, passed_along(): lax.ppermute(array, axis, [(i, (i + by) % peers) for i in range(peers)])  198 us
    reduce_scatter x1, waiting for transfers between devices, on_device(): lax.psum_scatter(carried.reshape(-1, width).astype(jnp.bfloat16), 'rep',...  89.5 us
    reduce_scatter x1, waiting for transfers between devices, on_device(): lax.psum_scatter(partial_value.reshape(-1, width), 'rep', scatter_dimensi...  87.8 us
    all_gather x1, blocking collectives, on_device(): panel = lax.all_gather(features, 'rep', axis=0, tiled=True)  50.9 us
    all_gather x1, blocking collectives, on_device(): lax.all_gather(back_rows, 'rep', axis=0, tiled=True)  47.7 us
  transfers between devices with their start and end apart: 24, of which 17 were waited for; matrix products, arithmetic and copies ran while one was open for 2% of the time, Pallas kernels for 0%

profile of v1, /device:TPU:6, one launch (start us, length us, event | category | flops | bytes accessed | tf_op | source)
XLA Modules:
  0.0 2079.5 jit_solution(13287652533729563896)
XLA Ops:
  7.2 50.9 %all_gather.6 = bf16[1024,256]{1,0:T(8,128)(2,1)S(1)} all-gather(bf16[128,256]{1,0:T(8,128)(2,1)} %param.9), channel_id=1, replica_groups=mesh['rep'=8,'blk'=64] {'rep'}, dimensions={0}, use_global_device_ids=true | all-gather | bytes 589824 | tf_op jit(solution)/shard_map/all_gather | solution.py:62
  58.1 32.2 %collective-permute-start = (bf16[1024,256]{1,0:T(8,128)(2,1)S(1)}, bf16[1024,256]{1,0:T(8,128)(2,1)S(1)}, u32[]{:S(2)}, u32[]{:S(2)}) collective-permute-start(bf16[1024,256]{1,0:T(8,128)(2,1)S(1)} %all_gather.6), channel_id=1, source_target_pairs={{0,8},{1,9},{2,10},{3,11},{4,12},{5,13},{6,14},{7,15},{8,16},{9,17... | collective-permute-start | bytes 1572872 | tf_op jit(solution)/shard_map/ppermute | solution.py:10
  91.9 19.1 collective-permute-done
  113.0 13.2 collective-permute-done.1
  129.5 11.4 collective-permute-done.2
  164.3 24.6 %collective-permute-start.5 = (bf16[8,128,256]{2,1,0:T(8,128)(2,1)}, bf16[8,128,256]{2,1,0:T(8,128)(2,1)}, u32[]{:S(2)}, u32[]{:S(2)}) collective-permute-start(bf16[8,128,256]{2,1,0:T(8,128)(2,1)} %collective-permute-done.4), channel_id=1, source_target_pairs={{0,1},{1,2},{2,3},{3,4},{4,5},{5,6},{6,7},{7,8},{8,9},{9,10},{10,1... | collective-permute-start | bytes 1572872 | tf_op jit(solution)/shard_map/ppermute | solution.py:10
  192.9 21.0 %collective-permute-start.6 = (bf16[8,128,256]{2,1,0:T(8,128)(2,1)}, bf16[8,128,256]{2,1,0:T(8,128)(2,1)}, u32[]{:S(2)}, u32[]{:S(2)}) collective-permute-start(bf16[8,128,256]{2,1,0:T(8,128)(2,1)} %collective-permute-done.5), channel_id=1, source_target_pairs={{0,1},{1,2},{2,3},{3,4},{4,5},{5,6},{6,7},{7,8},{8,9},{9,10},{10,1... | collective-permute-start | bytes 1572872 | tf_op jit(solution)/shard_map/ppermute | solution.py:10
  218.4 24.9 %collective-permute-start.7 = (bf16[8,128,256]{2,1,0:T(8,128)(2,1)}, bf16[8,128,256]{2,1,0:T(8,128)(2,1)}, u32[]{:S(2)}, u32[]{:S(2)}) collective-permute-start(bf16[8,128,256]{2,1,0:T(8,128)(2,1)} %collective-permute-done.6), channel_id=1, source_target_pairs={{0,1},{1,2},{2,3},{3,4},{4,5},{5,6},{6,7},{7,8},{8,9},{9,10},{10,1... | collective-permute-start | bytes 1572872 | tf_op jit(solution)/shard_map/ppermute | solution.py:10
  248.0 20.3 collective-permute-start.8
  273.0 24.9 %collective-permute-start.9 = (bf16[8,128,256]{2,1,0:T(8,128)(2,1)}, bf16[8,128,256]{2,1,0:T(8,128)(2,1)}, u32[]{:S(2)}, u32[]{:S(2)}) collective-permute-start(bf16[8,128,256]{2,1,0:T(8,128)(2,1)} %collective-permute-done.8), channel_id=1, source_target_pairs={{0,1},{1,2},{2,3},{3,4},{4,5},{5,6},{6,7},{7,8},{8,9},{9,10},{10,1... | collective-permute-start | bytes 1572872 | tf_op jit(solution)/shard_map/ppermute | solution.py:10
  307.9 87.8 %reduce-scatter.3.cloned.1.call-done = f32[128,256]{1,0:T(8,128)} async-done(((f32[1024,256]{1,0:T(8,128)}), f32[128,256]{1,0:T(8,128)}) %reduce-scatter.3.cloned.1.call-update) | async-done | bytes 131088 | tf_op jit(solution)/shard_map/reduce_scatter | solution.py:71
  397.6 47.7 %all_gather.7 = bf16[1024,256]{1,0:T(8,128)(2,1)S(1)} all-gather(bf16[128,256]{1,0:T(8,128)(2,1)S(1)} %convolution_convert_fusion), channel_id=1, replica_groups=mesh['rep'=8,'blk'=64] {'rep'}, dimensions={0}, use_global_device_ids=true | all-gather | bytes 589824 | tf_op jit(solution)/shard_map/all_gather | solution.py:83
  451.4 11.4 collective-permute-done.10
  471.6 33.1 %collective-permute-done.11 = f32[8,128,256]{2,0,1:T(8,128)} collective-permute-done((f32[8,128,256]{2,0,1:T(8,128)}, f32[8,128,256]{2,0,1:T(8,128)}, u32[]{:S(2)}, u32[]{:S(2)}) %collective-permute-start.11) | collective-permute-done | bytes 1048608 | tf_op jit(solution)/shard_map/ppermute | solution.py:10
  511.0 32.1 %collective-permute-done.12 = f32[8,128,256]{2,0,1:T(8,128)} collective-permute-done((f32[8,128,256]{2,0,1:T(8,128)}, f32[8,128,256]{2,0,1:T(8,128)}, u32[]{:S(2)}, u32[]{:S(2)}) %collective-permute-start.12) | collective-permute-done | bytes 1048608 | tf_op jit(solution)/shard_map/ppermute | solution.py:10
  549.5 38.3 %collective-permute-done.13 = f32[8,128,256]{2,0,1:T(8,128)} collective-permute-done((f32[8,128,256]{2,0,1:T(8,128)}, f32[8,128,256]{2,0,1:T(8,128)}, u32[]{:S(2)}, u32[]{:S(2)}) %collective-permute-start.13) | collective-permute-done | bytes 1048608 | tf_op jit(solution)/shard_map/ppermute | solution.py:10
  594.1 41.6 %collective-permute-done.14 = f32[8,128,256]{2,0,1:T(8,128)} collective-permute-done((f32[8,128,256]{2,0,1:T(8,128)}, f32[8,128,256]{2,0,1:T(8,128)}, u32[]{:S(2)}, u32[]{:S(2)}) %collective-permute-start.14) | collective-permute-done | bytes 1048608 | tf_op jit(solution)/shard_map/ppermute | solution.py:10
  642.1 45.2 %collective-permute-done.15 = f32[8,128,256]{2,0,1:T(8,128)} collective-permute-done((f32[8,128,256]{2,0,1:T(8,128)}, f32[8,128,256]{2,0,1:T(8,128)}, u32[]{:S(2)}, u32[]{:S(2)}) %collective-permute-start.15) | collective-permute-done | bytes 1048608 | tf_op jit(solution)/shard_map/ppermute | solution.py:10
  692.6 41.5 %collective-permute-done.16 = f32[8,128,256]{2,0,1:T(8,128)} collective-permute-done((f32[8,128,256]{2,0,1:T(8,128)S(1)}, f32[8,128,256]{2,0,1:T(8,128)}, u32[]{:S(2)}, u32[]{:S(2)}) %collective-permute-start.16) | collective-permute-done | bytes 1048608 | tf_op jit(solution)/shard_map/ppermute | solution.py:10
  735.5 11.1 collective-permute-start.17
  746.6 8.7 collective-permute-done.17
  773.9 205.1 %all-reduce.3.cloned.1.call-done = f32[256,256]{1,0:T(8,128)} async-done(((f32[256,256]{1,0:T(8,128)}), f32[256,256]{1,0:T(8,128)}) %all-reduce.3.cloned.1.call-update) | async-done | bytes 262160 | tf_op jit(solution)/shard_map/psum | solution.py:79
  980.3 1001.4 %all-reduce.5.cloned.1.call-done = f32[256,256]{1,0:T(8,128)} async-done(((f32[256,256]{1,0:T(8,128)}), f32[256,256]{1,0:T(8,128)}) %all-reduce.5.cloned.1.call-update) | async-done | bytes 262160 | tf_op jit(solution)/shard_map/psum | solution.py:79
  1983.4 89.5 %reduce-scatter.5.cloned.1.call-done = bf16[128,256]{1,0:T(8,128)(2,1)} async-done(((bf16[1024,256]{1,0:T(8,128)(2,1)}), bf16[128,256]{1,0:T(8,128)(2,1)}) %reduce-scatter.5.cloned.1.call-update) | async-done | bytes 65552 | tf_op jit(solution)/shard_map/reduce_scatter | solution.py:94
  (182 shorter events, 127.5 us)
Async XLA Ops:
  7.2 388.5 %reduce-scatter.3.cloned.1.call-start = ((), (), s32[]{:S(2)}) async-start(), calls=%async_computation.2 | async-start | bytes 1179648 | tf_op jit(solution)/shard_map/reduce_scatter | solution.py:71
  58.1 52.8 %collective-permute-start = (bf16[1024,256]{1,0:T(8,128)(2,1)S(1)}, bf16[1024,256]{1,0:T(8,128)(2,1)S(1)}, u32[]{:S(2)}, u32[]{:S(2)}) collective-permute-start(bf16[1024,256]{1,0:T(8,128)(2,1)S(1)} %all_gather.6), channel_id=1, source_target_pairs={{0,8},{1,9},{2,10},{3,11},{4,12},{5,13},{6,14},{7,15},{8,16},{9,17... | collective-permute-start | bytes 1572872 | tf_op jit(solution)/shard_map/ppermute | solution.py:10
  111.0 15.2 collective-permute-start.1
  126.3 14.6 collective-permute-start.2
  141.7 10.8 collective-permute-start.3
  152.5 11.7 collective-permute-start.4
  164.3 28.6 %collective-permute-start.5 = (bf16[8,128,256]{2,1,0:T(8,128)(2,1)}, bf16[8,128,256]{2,1,0:T(8,128)(2,1)}, u32[]{:S(2)}, u32[]{:S(2)}) collective-permute-start(bf16[8,128,256]{2,1,0:T(8,128)(2,1)} %collective-permute-done.4), channel_id=1, source_target_pairs={{0,1},{1,2},{2,3},{3,4},{4,5},{5,6},{6,7},{7,8},{8,9},{9,10},{10,1... | collective-permute-start | bytes 1572872 | tf_op jit(solution)/shard_map/ppermute | solution.py:10
  192.9 25.6 %collective-permute-start.6 = (bf16[8,128,256]{2,1,0:T(8,128)(2,1)}, bf16[8,128,256]{2,1,0:T(8,128)(2,1)}, u32[]{:S(2)}, u32[]{:S(2)}) collective-permute-start(bf16[8,128,256]{2,1,0:T(8,128)(2,1)} %collective-permute-done.5), channel_id=1, source_target_pairs={{0,1},{1,2},{2,3},{3,4},{4,5},{5,6},{6,7},{7,8},{8,9},{9,10},{10,1... | collective-permute-start | bytes 1572872 | tf_op jit(solution)/shard_map/ppermute | solution.py:10
  218.4 29.6 %collective-permute-start.7 = (bf16[8,128,256]{2,1,0:T(8,128)(2,1)}, bf16[8,128,256]{2,1,0:T(8,128)(2,1)}, u32[]{:S(2)}, u32[]{:S(2)}) collective-permute-start(bf16[8,128,256]{2,1,0:T(8,128)(2,1)} %collective-permute-done.6), channel_id=1, source_target_pairs={{0,1},{1,2},{2,3},{3,4},{4,5},{5,6},{6,7},{7,8},{8,9},{9,10},{10,1... | collective-permute-start | bytes 1572872 | tf_op jit(solution)/shard_map/ppermute | solution.py:10
  248.0 25.0 %collective-permute-start.8 = (bf16[8,128,256]{2,1,0:T(8,128)(2,1)}, bf16[8,128,256]{2,1,0:T(8,128)(2,1)}, u32[]{:S(2)}, u32[]{:S(2)}) collective-permute-start(bf16[8,128,256]{2,1,0:T(8,128)(2,1)} %collective-permute-done.7), channel_id=1, source_target_pairs={{0,1},{1,2},{2,3},{3,4},{4,5},{5,6},{6,7},{7,8},{8,9},{9,10},{10,1... | collective-permute-start | bytes 1572872 | tf_op jit(solution)/shard_map/ppermute | solution.py:10
  273.0 29.6 %collective-permute-start.9 = (bf16[8,128,256]{2,1,0:T(8,128)(2,1)}, bf16[8,128,256]{2,1,0:T(8,128)(2,1)}, u32[]{:S(2)}, u32[]{:S(2)}) collective-permute-start(bf16[8,128,256]{2,1,0:T(8,128)(2,1)} %collective-permute-done.8), channel_id=1, source_target_pairs={{0,1},{1,2},{2,3},{3,4},{4,5},{5,6},{6,7},{7,8},{8,9},{9,10},{10,1... | collective-permute-start | bytes 1572872 | tf_op jit(solution)/shard_map/ppermute | solution.py:10
  307.6 671.5 %all-reduce.3.cloned.1.call-start = ((), (), s32[]{:S(2)}) async-start(), calls=%async_computation.3 | async-start | bytes 524288 | tf_op jit(solution)/shard_map/psum | solution.py:79
  448.3 14.5 collective-permute-start.10
  465.8 38.9 %collective-permute-start.11 = (f32[8,128,256]{2,0,1:T(8,128)}, f32[8,128,256]{2,0,1:T(8,128)}, u32[]{:S(2)}, u32[]{:S(2)}) collective-permute-start(f32[8,128,256]{2,0,1:T(8,128)} %convolution_add_fusion), channel_id=1, source_target_pairs={{0,63},{1,0},{2,1},{3,2},{4,3},{5,4},{6,5},{7,6},{8,7},{9,8},{10,9... | collective-permute-start | bytes 3145736 | tf_op jit(solution)/shard_map/ppermute | solution.py:10
  507.1 36.0 %collective-permute-start.12 = (f32[8,128,256]{2,0,1:T(8,128)}, f32[8,128,256]{2,0,1:T(8,128)}, u32[]{:S(2)}, u32[]{:S(2)}) collective-permute-start(f32[8,128,256]{2,0,1:T(8,128)} %add.83), channel_id=1, source_target_pairs={{0,63},{1,0},{2,1},{3,2},{4,3},{5,4},{6,5},{7,6},{8,7},{9,8},{10,9... | collective-permute-start | bytes 3145736 | tf_op jit(solution)/shard_map/ppermute | solution.py:10
  545.6 42.3 %collective-permute-start.13 = (f32[8,128,256]{2,0,1:T(8,128)}, f32[8,128,256]{2,0,1:T(8,128)}, u32[]{:S(2)}, u32[]{:S(2)}) collective-permute-start(f32[8,128,256]{2,0,1:T(8,128)} %add.84), channel_id=1, source_target_pairs={{0,63},{1,0},{2,1},{3,2},{4,3},{5,4},{6,5},{7,6},{8,7},{9,8},{10,9... | collective-permute-start | bytes 3145736 | tf_op jit(solution)/shard_map/ppermute | solution.py:10
  590.3 45.5 %collective-permute-start.14 = (f32[8,128,256]{2,0,1:T(8,128)}, f32[8,128,256]{2,0,1:T(8,128)}, u32[]{:S(2)}, u32[]{:S(2)}) collective-permute-start(f32[8,128,256]{2,0,1:T(8,128)} %add.85), channel_id=1, source_target_pairs={{0,63},{1,0},{2,1},{3,2},{4,3},{5,4},{6,5},{7,6},{8,7},{9,8},{10,9... | collective-permute-start | bytes 3145736 | tf_op jit(solution)/shard_map/ppermute | solution.py:10
  638.2 49.1 %collective-permute-start.15 = (f32[8,128,256]{2,0,1:T(8,128)}, f32[8,128,256]{2,0,1:T(8,128)}, u32[]{:S(2)}, u32[]{:S(2)}) collective-permute-start(f32[8,128,256]{2,0,1:T(8,128)} %add.86), channel_id=1, source_target_pairs={{0,63},{1,0},{2,1},{3,2},{4,3},{5,4},{6,5},{7,6},{8,7},{9,8},{10,9... | collective-permute-start | bytes 3145736 | tf_op jit(solution)/shard_map/ppermute | solution.py:10
  688.7 45.4 %collective-permute-start.16 = (f32[8,128,256]{2,0,1:T(8,128)S(1)}, f32[8,128,256]{2,0,1:T(8,128)}, u32[]{:S(2)}, u32[]{:S(2)}) collective-permute-start(f32[8,128,256]{2,0,1:T(8,128)S(1)} %add.87), channel_id=1, source_target_pairs={{0,63},{1,0},{2,1},{3,2},{4,3},{5,4},{6,5},{7,6},{8,7},{9,8},{10,9... | collective-permute-start | bytes 3145736 | tf_op jit(solution)/shard_map/ppermute | solution.py:10
  735.5 19.8 collective-permute-start.17
  755.4 13.4 collective-permute-start.18
  769.0 210.1 %collective-permute-start.19 = (bf16[8,128,256]{2,0,1:T(8,128)(2,1)S(1)}, bf16[8,128,256]{2,0,1:T(8,128)(2,1)S(1)}, u32[]{:S(2)}, u32[]{:S(2)}) collective-permute-start(bf16[8,128,256]{2,0,1:T(8,128)(2,1)S(1)} %fusion.25), channel_id=1, source_target_pairs={{0,32},{1,33},{2,34},{3,35},{4,36},{5,37},{6,38},{7,39},{8,40},{9,... | collective-permute-start | bytes 1572872 | tf_op jit(solution)/shard_map/ppermute | solution.py:10
  773.8 1207.9 %all-reduce.5.cloned.1.call-start = ((), (), s32[]{:S(2)}) async-start(), calls=%async_computation.4 | async-start | bytes 524288 | tf_op jit(solution)/shard_map/psum | solution.py:79
  979.1 1093.9 %reduce-scatter.5.cloned.1.call-start = ((), (), s32[]{:S(2)}) async-start(), calls=%async_computation.5 | async-start | bytes 589824 | tf_op jit(solution)/shard_map/reduce_scatter | solution.py:94
  (12 other events, 601.9 us)
Sparse Core Ops, SparseCore 0:
  307.7 87.8 reduce-scatter.2
  774.0 205.0 all-reduce.2
  982.2 999.4 all-reduce.4
  1985.0 87.9 reduce-scatter.4
